TPU v7x, 32 devices: a whole 2x2x4 slice. The times are simulated.
32 devices in a mesh: group: 2 (over x), blk: 8 (over z, y), ulysses: 2 (over core).
Axes of the slice: x: 2, y: 2, z: 4, core: 2. Of those that a mesh axis runs over, the one named last changes fastest.
Arguments:
- query_int: bfloat16 [4096, 8192], P(('group', 'blk', 'ulysses')), parts along dimension 0, may hold values from -127 to 127, as said below
- key_int: bfloat16 [4096, 1024], P(('group', 'blk', 'ulysses')), parts along dimension 0, may hold values from -127 to 127, as said below
- values: bfloat16 [4096, 1024], P(('group', 'blk', 'ulysses')), parts along dimension 0, may hold values from -6 to 6
- query_scale: bfloat16 [32, 64], P(('group', 'blk')), parts along dimension 0, may hold values from 0.001 to 0.02
- key_scale: bfloat16 [32, 8], P('group'), parts along dimension 0, may hold values from 0.002 to 0.04
- verticals: int32 [16, 8], P('group'), parts along dimension 0, may hold values from 0 to 15, as said below
- slashes: int32 [16, 8], P('group'), parts along dimension 0, may hold values from 0 to 8, as said below
Outputs:
- attention: bfloat16 [4096, 8192], P(('group', 'blk', 'ulysses')), parts along dimension 0
There are 2 independent parts, one for each index of `group`. A program takes and returns all parts, laid end to end along the dimension named above; each array names one. Nothing has to cross between parts.
Inputs may be any that keep to these rules, and one draw needn't show every extreme that they name: `query_int`: integer values. `key_int`: integer values. `verticals`: each row holds 8 distinct key blocks, block 0 among them. `slashes`: each row holds 8 distinct offsets, 0 among them.
All inputs are finite; a program needn't handle non-finite values.
Results may differ from a plain program's by a relative error of at most 0.0019.
Values may be sent and summed in bfloat16 or wider, within the bound.
A program may use at most 128 MiB of HBM per device.

v0:
```python
import jax
import jax.numpy as jnp
from jax import lax
from jax.sharding import PartitionSpec as P

DH = 128
BLOCK = 128
FLOOR_SCORE = -1e30


def block_table(verticals, slashes, first_block, block_count):
    blocks = first_block + jnp.arange(block_count, dtype=jnp.int32)
    slash_keys = blocks[:, None, None] - slashes[None, :, :]
    slash_live = slash_keys >= 0
    vert_keys = jnp.broadcast_to(verticals[None, :, :], (block_count,) + verticals.shape)
    clashes = jnp.any(
        (vert_keys[:, :, :, None] == slash_keys[:, :, None, :]) & slash_live[:, :, None, :], axis=3
    )
    vert_live = (vert_keys <= blocks[:, None, None]) & jnp.logical_not(clashes)
    return (
        jnp.concatenate([vert_keys, slash_keys], axis=2),
        jnp.concatenate([vert_live, slash_live], axis=2),
        blocks,
    )


def gather_blocks(buffer, positions, groups):
    shaped = buffer.reshape(buffer.shape[0] // BLOCK, BLOCK, groups, DH)
    heads_at = jnp.arange(groups, dtype=jnp.int32)[None, :, None]
    return shaped[positions, :, heads_at, :]


def attend_group(pieces):
    query_block, query_scales, key_blocks, value_blocks, key_scales, live_slots, diagonal = pieces
    dots = jnp.einsum("tpd,nsd->ptns", query_block, key_blocks, preferred_element_type=jnp.float32)
    scores = dots * query_scales[:, None, None, None] * key_scales[None, None, :, None]
    width = query_block.shape[0]
    causal = jnp.arange(width)[None, :] <= jnp.arange(width)[:, None]
    allowed = live_slots[None, None, :, None] & (
        jnp.logical_not(diagonal)[None, None, :, None] | causal[None, :, None, :]
    )
    masked = jnp.where(allowed, scores, FLOOR_SCORE)
    largest = jnp.max(masked, axis=(2, 3), keepdims=True)
    weights = jnp.where(allowed, jnp.exp(masked - largest), 0.0)
    totals = jnp.sum(weights, axis=(2, 3))
    numer = jnp.einsum(
        "ptns,nsd->tpd",
        weights.astype(jnp.bfloat16),
        value_blocks,
        preferred_element_type=jnp.float32,
    )
    return (numer / jnp.transpose(totals, (1, 0))[:, :, None]).astype(jnp.bfloat16)


def attend_block(pieces):
    query_block, query_scales, key_blocks, value_blocks, key_scales, live_slots, diagonal = pieces
    by_group = lax.map(
        attend_group,
        (
            jnp.transpose(query_block, (1, 0, 2, 3)),
            query_scales,
            key_blocks,
            value_blocks,
            key_scales,
            live_slots,
            diagonal,
        ),
    )
    return jnp.transpose(by_group, (1, 0, 2, 3))


def local(query_int, key_int, values, query_scale, key_scale, verticals, slashes):
    query_here, key_here, value_here = (
        lax.all_to_all(query_int, "ulysses", split_axis=1, concat_axis=0, tiled=True),
        lax.all_to_all(key_int, "ulysses", split_axis=1, concat_axis=0, tiled=True),
        lax.all_to_all(values, "ulysses", split_axis=1, concat_axis=0, tiled=True),
    )
    half_index = lax.axis_index("ulysses")
    span_index = lax.axis_index("blk")
    span_rows = query_here.shape[0]
    block_count = span_rows // BLOCK
    heads_here = query_here.shape[1] // DH
    groups_here = key_here.shape[1] // DH
    per_group = heads_here // groups_here
    first_block = span_index * block_count
    group_ids = half_index * groups_here + jnp.arange(groups_here, dtype=jnp.int32)
    query_scales = lax.dynamic_slice_in_dim(query_scale, half_index * heads_here, heads_here, 1)
    query_scales = query_scales.astype(jnp.float32).reshape(block_count, groups_here, per_group)
    vert_here = lax.dynamic_slice_in_dim(verticals, half_index * groups_here, groups_here, 0)
    slash_here = lax.dynamic_slice_in_dim(slashes, half_index * groups_here, groups_here, 0)
    block_keys, live_slots, blocks = block_table(vert_here, slash_here, first_block, block_count)
    total_blocks = key_scale.shape[0]
    clipped = jnp.clip(block_keys, 0, total_blocks - 1)
    key_scales = key_scale[clipped, group_ids[None, :, None]].astype(jnp.float32)
    key_all, value_all = (
        lax.all_gather(key_here, "blk", axis=0, tiled=True),
        lax.all_gather(value_here, "blk", axis=0, tiled=True),
    )
    key_blocks = gather_blocks(key_all, clipped, groups_here)
    value_blocks = gather_blocks(value_all, clipped, groups_here)
    diagonal = block_keys == blocks[:, None, None]
    query_blocks = query_here.reshape(block_count, BLOCK, groups_here, per_group, DH)
    outputs = lax.map(
        attend_block,
        (query_blocks, query_scales, key_blocks, value_blocks, key_scales, live_slots, diagonal),
    )
    merged = outputs.reshape(span_rows, heads_here * DH)
    return lax.all_to_all(merged, "ulysses", split_axis=0, concat_axis=1, tiled=True)


def solution(mesh):
    in_specs = (
        P(("group", "blk", "ulysses"), None),
        P(("group", "blk", "ulysses"), None),
        P(("group", "blk", "ulysses"), None),
        P(("group", "blk"), None),
        P("group", None),
        P("group", None),
        P("group", None),
    )
    out_specs = P(("group", "blk", "ulysses"), None)
    return jax.shard_map(local, mesh=mesh, in_specs=in_specs, out_specs=out_specs, check_vma=False)
```

profile of v0, /device:TPU:0, one launch (start us, length us, event | category | flops | bytes accessed | tf_op | source)
XLA Modules:
  0.0 241.5 jit_solution(8448017913891180040)
XLA Ops:
  6.5 1.3 copy.58
  7.8 3.9 %all_to_all.73 = bf16[128,2,512]{0,2,1:T(8,128)(2,1)S(1)} all-to-all(bf16[128,2,512]{0,2,1:T(8,128)(2,1)S(1)} %bitcast.156), channel_id=1, replica_groups=mesh['group'=2,'blk'=8,'ulysses'=2] {'ulysses'}, dimensions={1} | all-to-all | bytes 524288 | tf_op jit(solution)/shard_map/all_to_all | solution.py:75
  11.8 0.8 copy.59
  12.7 1.1 copy.62
  13.8 3.9 %all_to_all.74 = bf16[128,2,512]{0,2,1:T(8,128)(2,1)S(1)} all-to-all(bf16[128,2,512]{0,2,1:T(8,128)(2,1)S(1)} %bitcast.157), channel_id=1, replica_groups=mesh['group'=2,'blk'=8,'ulysses'=2] {'ulysses'}, dimensions={1} | all-to-all | bytes 524288 | tf_op jit(solution)/shard_map/all_to_all | solution.py:76
  17.7 0.9 copy.63
  18.7 2.4 %copy.57 = bf16[128,8192]{0,1:T(8,128)(2,1)} copy(bf16[128,8192]{1,0:T(8,128)(2,1)S(1)} %copy-done.1) | data formatting | bytes 4194304 | tf_op args[0]
  21.1 5.0 %all-to-all-start = ((bf16[128,2,4096]{0,2,1:T(8,128)(2,1)}), bf16[128,2,4096]{0,2,1:T(8,128)(2,1)}, u32[]{:S(2)}, u32[]{:S(2)}) async-start(bf16[128,2,4096]{0,2,1:T(8,128)(2,1)} %bitcast.27), calls=%async_computation | async-start | bytes 4194304 | tf_op jit(solution)/shard_map/all_to_all | solution.py:74
  26.6 1.5 gather_fusion.2
  28.4 0.3 and_reduce_fusion
  28.9 35.7 %all-gather.3.cloned.1.call-done = bf16[2048,512]{1,0:T(8,128)(2,1)} async-done(((bf16[256,512]{1,0:T(8,128)(2,1)}), bf16[2048,512]{1,0:T(8,128)(2,1)}) %all-gather.3.cloned.1.call-update) | async-done | bytes 2097168 | tf_op jit(solution)/shard_map/all_gather | solution.py:96
  64.6 4.0 %reshape.141 = bf16[16,128,4,128]{3,2,1,0:T(4,128)(2,1)} reshape(bf16[2048,512]{1,0:T(8,128)(2,1)} %all-gather.3.cloned.1.call-done) | data formatting | bytes 4194304 | tf_op jit(solution)/shard_map/reshape | solution.py:28
  68.6 2.1 copy.61
  70.7 43.7 %all-gather.5.cloned.1.call-done = bf16[2048,512]{1,0:T(8,128)(2,1)} async-done(((bf16[256,512]{1,0:T(8,128)(2,1)}), bf16[2048,512]{1,0:T(8,128)(2,1)}) %all-gather.5.cloned.1.call-update) | async-done | bytes 2097168 | tf_op jit(solution)/shard_map/all_gather | solution.py:97
  114.4 4.0 %reshape.142 = bf16[16,128,4,128]{3,2,1,0:T(4,128)(2,1)} reshape(bf16[2048,512]{1,0:T(8,128)(2,1)} %all-gather.5.cloned.1.call-done) | data formatting | bytes 4194304 | tf_op jit(solution)/shard_map/reshape | solution.py:28
  118.3 3.5 %copy.65 = bf16[16,128,4,128]{3,1,2,0:T(8,128)(2,1)} copy(bf16[16,128,4,128]{3,2,1,0:T(4,128)(2,1)} %reshape.142) | data formatting | bytes 4194304 | tf_op jit(solution)/shard_map/reshape | solution.py:28
  121.8 3.1 %gather_fusion = bf16[128,128,128]{2,1,0:T(8,128)(2,1)} fusion(bf16[16,128,4,128]{3,1,2,0:T(8,128)(2,1)S(1)} %copy.61, s32[128]{0:T(128)S(1)} %reshape.118), kind=kCustom, calls=%fused_computation | custom fusion | bytes 8389632 | tf_op jit(solution)/shard_map/gather | solution.py:30
  124.9 4.7 %gather_fusion.1 = bf16[128,128,128]{2,1,0:T(8,128)(2,1)} fusion(bf16[16,128,4,128]{3,1,2,0:T(8,128)(2,1)} %copy.65, s32[128]{0:T(128)S(1)} %reshape.118), kind=kCustom, calls=%fused_computation.1 | custom fusion | bytes 8389632 | tf_op jit(solution)/shard_map/gather | solution.py:30
  129.6 89.9 %while.21 = (s32[]{:T(128)}, bf16[2,128,4,8,128]{1,4,3,2,0:T(8,128)(2,1)}, bf16[2,128,4,8,128]{1,4,3,2,0:T(8,128)(2,1)}, f32[2,4,8]{2,1,0:T(4,128)S(1)}, bf16[2,...) while((s32[]{:T(128)}, ...), condition=%wide.region_6.7_spmd, body=%wide.region_1.6_spmd.sunk | while | flops 1108097024 | bytes 46721236 | solution.py:103
  129.6 1.7 constant_dynamic-slice_fusion.13
  131.3 2.6 %copy.84 = bf16[1,4,16,128,128]{3,4,2,1,0:T(8,128)(2,1)} copy(bf16[1,4,16,128,128]{4,3,2,1,0:T(8,128)(2,1)S(1)} %constant_dynamic-slice_fusion.13) | data formatting | bytes 4194304 | tf_op jit(solution)/shard_map/while/body/jit(dynamic_index_in_dim)/dynamic_slice | solution.py:103
  133.9 1.3 constant_dynamic-slice_fusion.14
  135.2 1.4 copy.85
  136.6 1.7 dynamic-slice_bitcast_fusion.6
  138.3 35.1 %while.22 = (s32[]{:T(128)}, bf16[4,128,8,128]{1,3,2,0:T(8,128)(2,1)S(1)}, bf16[4,16,128,128]{2,3,1,0:T(8,128)(2,1)}, pred[4,16]{1,0:T(4,128)(4,1)S(1)}, pred[4,...) while((s32[]{:T(128)}, ...), condition=%wide.region_5.5_spmd, body=%wide.region_2.4_spmd.sunk | while | flops 1108097024 | bytes 27845104 | solution.py:57
  138.4 0.2 or_and_fusion.2
  138.7 2.4 fusion.58
  141.1 2.4 fusion.59
  143.5 3.6 %fusion.60 = bf16[4,128,8,128]{1,3,2,0:T(8,128)(2,1)S(1)} fusion(bf16[4,128,8,128]{1,3,2,0:T(8,128)(2,1)S(1)} %get-tuple-element.347, s32[]{:T(128)} %get-tuple-element.346, f32[16,128,128,8]{2,1,3,0:T(8,128)S(1)} %get-tuple-element.334, f32[8,128]{1,0:T(8,128)S(1)} %get-tuple-element.335, f32[16]{0:T(128)S(1)} %fusion.55, f32[8]{0:T(128)S(1)} %fusion.56, ...), kind=kOutput, calls=%fused_computation.14.clone.1 | convolution fusion | flops 549715968 | bytes 9447424 | tf_op jit(solution)/shard_map/while/body/eval_jaxpr/while/body/eval_jaxpr/ptns,nsd->tpd/dot_general | solution.py:46
  147.2 0.2 or_and_fusion.2
  147.5 2.4 fusion.58
  149.9 2.4 fusion.59
  152.3 3.6 %fusion.60 = bf16[4,128,8,128]{1,3,2,0:T(8,128)(2,1)S(1)} fusion(bf16[4,128,8,128]{1,3,2,0:T(8,128)(2,1)S(1)} %get-tuple-element.347, s32[]{:T(128)} %get-tuple-element.346, f32[16,128,128,8]{2,1,3,0:T(8,128)S(1)} %get-tuple-element.334, f32[8,128]{1,0:T(8,128)S(1)} %get-tuple-element.335, f32[16]{0:T(128)S(1)} %fusion.55, f32[8]{0:T(128)S(1)} %fusion.56, ...), kind=kOutput, calls=%fused_computation.14.clone.1 | convolution fusion | flops 549715968 | bytes 9447424 | tf_op jit(solution)/shard_map/while/body/eval_jaxpr/while/body/eval_jaxpr/ptns,nsd->tpd/dot_general | solution.py:46
  156.2 2.4 fusion.58
  158.6 2.4 fusion.59
  161.1 3.6 %fusion.60 = bf16[4,128,8,128]{1,3,2,0:T(8,128)(2,1)S(1)} fusion(bf16[4,128,8,128]{1,3,2,0:T(8,128)(2,1)S(1)} %get-tuple-element.347, s32[]{:T(128)} %get-tuple-element.346, f32[16,128,128,8]{2,1,3,0:T(8,128)S(1)} %get-tuple-element.334, f32[8,128]{1,0:T(8,128)S(1)} %get-tuple-element.335, f32[16]{0:T(128)S(1)} %fusion.55, f32[8]{0:T(128)S(1)} %fusion.56, ...), kind=kOutput, calls=%fused_computation.14.clone.1 | convolution fusion | flops 549715968 | bytes 9447424 | tf_op jit(solution)/shard_map/while/body/eval_jaxpr/while/body/eval_jaxpr/ptns,nsd->tpd/dot_general | solution.py:46
  164.7 0.2 or_and_fusion.2
  165.0 2.4 fusion.58
  167.4 2.4 fusion.59
  169.8 3.6 %fusion.60 = bf16[4,128,8,128]{1,3,2,0:T(8,128)(2,1)S(1)} fusion(bf16[4,128,8,128]{1,3,2,0:T(8,128)(2,1)S(1)} %get-tuple-element.347, s32[]{:T(128)} %get-tuple-element.346, f32[16,128,128,8]{2,1,3,0:T(8,128)S(1)} %get-tuple-element.334, f32[8,128]{1,0:T(8,128)S(1)} %get-tuple-element.335, f32[16]{0:T(128)S(1)} %fusion.55, f32[8]{0:T(128)S(1)} %fusion.56, ...), kind=kOutput, calls=%fused_computation.14.clone.1 | convolution fusion | flops 549715968 | bytes 9447424 | tf_op jit(solution)/shard_map/while/body/eval_jaxpr/while/body/eval_jaxpr/ptns,nsd->tpd/dot_general | solution.py:46
  173.5 1.0 bitcast_dynamic-update-slice_fusion.2
  174.5 1.7 constant_dynamic-slice_fusion.13
  176.2 2.6 %copy.84 = bf16[1,4,16,128,128]{3,4,2,1,0:T(8,128)(2,1)} copy(bf16[1,4,16,128,128]{4,3,2,1,0:T(8,128)(2,1)S(1)} %constant_dynamic-slice_fusion.13) | data formatting | bytes 4194304 | tf_op jit(solution)/shard_map/while/body/jit(dynamic_index_in_dim)/dynamic_slice | solution.py:103
  178.8 1.3 constant_dynamic-slice_fusion.14
  180.1 1.4 copy.85
  181.5 1.7 dynamic-slice_bitcast_fusion.6
  183.3 35.1 %while.22 = (s32[]{:T(128)}, bf16[4,128,8,128]{1,3,2,0:T(8,128)(2,1)S(1)}, bf16[4,16,128,128]{2,3,1,0:T(8,128)(2,1)}, pred[4,16]{1,0:T(4,128)(4,1)S(1)}, pred[4,...) while((s32[]{:T(128)}, ...), condition=%wide.region_5.5_spmd, body=%wide.region_2.4_spmd.sunk | while | flops 1108097024 | bytes 27845104 | solution.py:57
  183.6 2.4 fusion.58
  186.0 2.4 fusion.59
  188.4 3.6 %fusion.60 = bf16[4,128,8,128]{1,3,2,0:T(8,128)(2,1)S(1)} fusion(bf16[4,128,8,128]{1,3,2,0:T(8,128)(2,1)S(1)} %get-tuple-element.347, s32[]{:T(128)} %get-tuple-element.346, f32[16,128,128,8]{2,1,3,0:T(8,128)S(1)} %get-tuple-element.334, f32[8,128]{1,0:T(8,128)S(1)} %get-tuple-element.335, f32[16]{0:T(128)S(1)} %fusion.55, f32[8]{0:T(128)S(1)} %fusion.56, ...), kind=kOutput, calls=%fused_computation.14.clone.1 | convolution fusion | flops 549715968 | bytes 9447424 | tf_op jit(solution)/shard_map/while/body/eval_jaxpr/while/body/eval_jaxpr/ptns,nsd->tpd/dot_general | solution.py:46
  192.4 2.4 fusion.58
  194.8 2.4 fusion.59
  197.2 3.6 %fusion.60 = bf16[4,128,8,128]{1,3,2,0:T(8,128)(2,1)S(1)} fusion(bf16[4,128,8,128]{1,3,2,0:T(8,128)(2,1)S(1)} %get-tuple-element.347, s32[]{:T(128)} %get-tuple-element.346, f32[16,128,128,8]{2,1,3,0:T(8,128)S(1)} %get-tuple-element.334, f32[8,128]{1,0:T(8,128)S(1)} %get-tuple-element.335, f32[16]{0:T(128)S(1)} %fusion.55, f32[8]{0:T(128)S(1)} %fusion.56, ...), kind=kOutput, calls=%fused_computation.14.clone.1 | convolution fusion | flops 549715968 | bytes 9447424 | tf_op jit(solution)/shard_map/while/body/eval_jaxpr/while/body/eval_jaxpr/ptns,nsd->tpd/dot_general | solution.py:46
  201.2 2.4 fusion.58
  203.6 2.4 fusion.59
  206.0 3.6 %fusion.60 = bf16[4,128,8,128]{1,3,2,0:T(8,128)(2,1)S(1)} fusion(bf16[4,128,8,128]{1,3,2,0:T(8,128)(2,1)S(1)} %get-tuple-element.347, s32[]{:T(128)} %get-tuple-element.346, f32[16,128,128,8]{2,1,3,0:T(8,128)S(1)} %get-tuple-element.334, f32[8,128]{1,0:T(8,128)S(1)} %get-tuple-element.335, f32[16]{0:T(128)S(1)} %fusion.55, f32[8]{0:T(128)S(1)} %fusion.56, ...), kind=kOutput, calls=%fused_computation.14.clone.1 | convolution fusion | flops 549715968 | bytes 9447424 | tf_op jit(solution)/shard_map/while/body/eval_jaxpr/while/body/eval_jaxpr/ptns,nsd->tpd/dot_general | solution.py:46
  209.9 2.4 fusion.58
  212.3 2.4 fusion.59
  214.8 3.6 %fusion.60 = bf16[4,128,8,128]{1,3,2,0:T(8,128)(2,1)S(1)} fusion(bf16[4,128,8,128]{1,3,2,0:T(8,128)(2,1)S(1)} %get-tuple-element.347, s32[]{:T(128)} %get-tuple-element.346, f32[16,128,128,8]{2,1,3,0:T(8,128)S(1)} %get-tuple-element.334, f32[8,128]{1,0:T(8,128)S(1)} %get-tuple-element.335, f32[16]{0:T(128)S(1)} %fusion.55, f32[8]{0:T(128)S(1)} %fusion.56, ...), kind=kOutput, calls=%fused_computation.14.clone.1 | convolution fusion | flops 549715968 | bytes 9447424 | tf_op jit(solution)/shard_map/while/body/eval_jaxpr/while/body/eval_jaxpr/ptns,nsd->tpd/dot_general | solution.py:46
  218.4 1.0 bitcast_dynamic-update-slice_fusion.2
  219.4 2.9 %copy.79 = bf16[2,128,4096]{2,1,0:T(8,128)(2,1)S(1)} copy(bf16[2,128,4096]{1,2,0:T(8,128)(2,1)} %bitcast.151) | data formatting | bytes 4194304 | tf_op jit(solution)/shard_map/all_to_all | solution.py:108
  222.4 6.3 %all_to_all.75 = bf16[2,128,4096]{2,1,0:T(8,128)(2,1)} all-to-all(bf16[2,128,4096]{2,1,0:T(8,128)(2,1)S(1)} %copy.79), channel_id=1, replica_groups=mesh['group'=2,'blk'=8,'ulysses'=2] {'ulysses'}, dimensions={0} | all-to-all | bytes 4194304 | tf_op jit(solution)/shard_map/all_to_all | solution.py:108
  228.7 3.1 %copy.69 = bf16[2,128,4096]{1,2,0:T(8,128)(2,1)S(1)} copy(bf16[2,128,4096]{2,1,0:T(8,128)(2,1)} %all_to_all.75) | data formatting | bytes 4194304 | tf_op jit(solution)/shard_map/all_to_all | solution.py:108
  231.8 2.9 %copy.70 = bf16[128,8192]{1,0:T(8,128)(2,1)} copy(bf16[128,8192]{0,1:T(8,128)(2,1)S(1)} %bitcast.149) | data formatting | bytes 4194304 | tf_op jit(solution)/shard_map/all_to_all | solution.py:108
  (77 shorter events, 2.6 us)
Async XLA Ops:
  6.5 20.0 %copy-start = (bf16[16,8]{0,1:T(8,128)(2,1)S(1)}, bf16[16,8]{0,1:T(8,128)(2,1)}, u32[]{:S(2)}) copy-start(bf16[16,8]{0,1:T(8,128)(2,1)} %param.15) | copy-start | bytes 772
  6.5 12.1 %copy-start.1 = (bf16[128,8192]{1,0:T(8,128)(2,1)S(1)}, bf16[128,8192]{1,0:T(8,128)(2,1)}, u32[]{:S(2)}) copy-start(bf16[128,8192]{1,0:T(8,128)(2,1)} %param.11) | copy-start | bytes 6291460
  6.5 58.1 %all-gather.3.cloned.1.call-start = ((), (), s32[]{:S(2)}) async-start(), calls=%async_computation.4 | async-start | bytes 2359296 | tf_op jit(solution)/shard_map/all_gather | solution.py:96
  12.6 101.7 %all-gather.5.cloned.1.call-start = ((), (), s32[]{:S(2)}) async-start(), calls=%async_computation.5 | async-start | bytes 2359296 | tf_op jit(solution)/shard_map/all_gather | solution.py:97
  18.6 7.6 %copy-start.2 = (s32[8,8]{1,0:T(8,128)S(1)}, s32[8,8]{1,0:T(8,128)}, u32[]{:S(2)}) copy-start(s32[8,8]{1,0:T(8,128)} %param.17) | copy-start | bytes 772
  18.7 7.6 %copy-start.3 = (s32[8,8]{1,0:T(8,128)S(1)}, s32[8,8]{1,0:T(8,128)}, u32[]{:S(2)}) copy-start(s32[8,8]{1,0:T(8,128)} %param.16) | copy-start | bytes 772
  21.1 7.1 %copy-start.4 = (bf16[2,64]{1,0:T(2,128)(2,1)S(1)}, bf16[2,64]{1,0:T(2,128)(2,1)}, u32[]{:S(2)}) copy-start(bf16[2,64]{1,0:T(2,128)(2,1)} %param.14) | copy-start | bytes 772
  21.1 108.5 %all-to-all-start = ((bf16[128,2,4096]{0,2,1:T(8,128)(2,1)}), bf16[128,2,4096]{0,2,1:T(8,128)(2,1)}, u32[]{:S(2)}, u32[]{:S(2)}) async-start(bf16[128,2,4096]{0,2,1:T(8,128)(2,1)} %bitcast.27), calls=%async_computation | async-start | bytes 4194304 | tf_op jit(solution)/shard_map/all_to_all | solution.py:74
Sparse Core Ops, SparseCore 0:
  12.8 51.8 all-gather.2
  66.7 47.5 all-gather.4
where the time goes:
time: 243 us; the launch traced here: 242 us
  waiting for transfers between devices  79.3 us (33%)
  local copies, waits for them, and re-layouts  58.4 us (24%)
  matrix products  48.1 us (20%)
  other arithmetic  22.2 us (9%)
  blocking collectives  14.2 us (6%)
  between operations  13.6 us (6%)
  starting transfers between devices  5.08 us (2%)
    all_gather x1, waiting for transfers between devices, local(): lax.all_gather(value_here, 'blk', axis=0, tiled=True)  43.7 us
    all_gather x1, waiting for transfers between devices, local(): lax.all_gather(key_here, 'blk', axis=0, tiled=True)  35.7 us
    dot_general x8, matrix products, attend_group(): jnp.einsum('ptns,nsd->tpd', weights.astype(jnp.bfloat16), value_blocks, p...  28.8 us
    reduce_sum x8, other arithmetic, attend_group(): totals = jnp.sum(weights, axis=(2, 3))  19.3 us
    dot_general x8, matrix products, attend_group(): jnp.einsum('tpd,nsd->ptns', query_block, key_blocks, preferred_element_ty...  19.2 us
    dynamic_slice x8, local copies, waits for them, and re-layouts, local(): lax.map(attend_block, (query_blocks, query_scales, key_blocks, value_bloc...  14 us
    reshape x4, local copies, waits for them, and re-layouts, gather_blocks(): shaped = buffer.reshape(buffer.shape[0] // BLOCK, BLOCK, groups, DH)  13.5 us
    all_to_all x3, local copies, waits for them, and re-layouts, local(): lax.all_to_all(merged, 'ulysses', split_axis=0, concat_axis=1, tiled=True)  8.94 us
  transfers between devices with their start and end apart: 3, of which 2 were waited for; matrix products, arithmetic and copies ran while one was open for 12% of the time, Pallas kernels for 0%

commit v1 on v0

--- a/solution.py
+++ b/solution.py
@@ -6,6 +6,28 @@
 DH = 128
 BLOCK = 128
 FLOOR_SCORE = -1e30
+
+
+def laid_out(tiles, dim):
+    tiles = jnp.moveaxis(tiles, 0, dim)
+    dims = tiles.shape
+    return tiles.reshape(*dims[:dim], dims[dim] * dims[dim + 1], *dims[dim + 2 :])
+
+
+def collect(value, axis, dim):
+    size = lax.axis_size(axis)
+    pairs = [(i, (i + 1) % size) for i in range(size)]
+    back = [(b, a) for a, b in pairs]
+    lower, upper = ([], [])
+    for step in range(size - 1):
+        if step % 2 == 0:
+            lower.append(lax.ppermute(lower[-1] if lower else value, axis, pairs))
+        else:
+            upper.append(lax.ppermute(upper[-1] if upper else value, axis, back))
+    parts = jnp.stack([*lower[::-1], value, *upper])
+    shift = lax.axis_index(axis) - len(lower)
+    parts = parts[(jnp.arange(size) - shift) % size]
+    return laid_out(parts, dim)
 
 
 def block_table(verticals, slashes, first_block, block_count):
@@ -93,7 +115,7 @@
     clipped = jnp.clip(block_keys, 0, total_blocks - 1)
     key_scales = key_scale[clipped, group_ids[None, :, None]].astype(jnp.float32)
     key_all, value_all = (
-        lax.all_gather(key_here, "blk", axis=0, tiled=True),
+        collect(key_here, "blk", 0),
         lax.all_gather(value_here, "blk", axis=0, tiled=True),
     )
     key_blocks = gather_blocks(key_all, clipped, groups_here)

time: 243 us -> 221 us (0.909)
  waiting for transfers between devices: 79.3 us -> 36.3 us
  starting transfers between devices: 5.08 us -> 23.5 us
  local copies, waits for them, and re-layouts: 58.4 us -> 61.1 us
    all_gather x1, waiting for transfers between devices: 43.7 us -> 0.01 us  [local(): lax.all_gather(value_here, 'blk', axis=0, tiled=True)]
    ppermute x0 -> x7, waiting for transfers between devices: none -> 36.3 us  [the longest x4 36.3 us: collect(): lower.append(lax.ppermute(lower[-1] if lower else value, axis, pairs))]
    all_gather x1 -> x0, waiting for transfers between devices: 35.7 us -> none  [local(): lax.all_gather(key_here, 'blk', axis=0, tiled=True)]
    ppermute x0 -> x7, starting transfers between devices: none -> 18.5 us  [the longest x3 12.9 us: collect(): upper.append(lax.ppermute(upper[-1] if upper else value, axis, back))]
    reshape x4 -> x2, local copies, waits for them, and re-layouts: 13.5 us -> 6.17 us  [gather_blocks(): shaped = buffer.reshape(buffer.shape[0] // BLOCK, BLOCK, groups, DH)]
    unnamed x13 -> x20, local copies, waits for them, and re-layouts: 4.85 us -> 9.93 us
    another operation x0 -> x3, local copies, waits for them, and re-layouts: none -> 5.02 us  [the longest x2 4.26 us: gather_blocks(): shaped = buffer.reshape(buffer.shape[0] // BLOCK, BLOCK, groups, DH)]
  transfers between devices with their start and end apart: 3 -> 9, of which waited for: 2 -> 3; matrix products, arithmetic and copies ran while one was open for 12% -> 15% of each run, Pallas kernels for 0% -> 0%
where the time goes in v1:
time: 221 us; the launch traced here: 220 us
  local copies, waits for them, and re-layouts  61.1 us (28%)
  matrix products  48.1 us (22%)
  waiting for transfers between devices  36.3 us (16%)
  starting transfers between devices  23.5 us (11%)
  other arithmetic  22.2 us (10%)
  blocking collectives  14.2 us (6%)
  between operations  13.6 us (6%)
    ppermute x4, waiting for transfers between devices, collect(): lower.append(lax.ppermute(lower[-1] if lower else value, axis, pairs))  36.3 us
    dot_general x8, matrix products, attend_group(): jnp.einsum('ptns,nsd->tpd', weights.astype(jnp.bfloat16), value_blocks, p...  28.8 us
    reduce_sum x8, other arithmetic, attend_group(): totals = jnp.sum(weights, axis=(2, 3))  19.3 us
    dot_general x8, matrix products, attend_group(): jnp.einsum('tpd,nsd->ptns', query_block, key_blocks, preferred_element_ty...  19.2 us
    dynamic_slice x8, local copies, waits for them, and re-layouts, local(): lax.map(attend_block, (query_blocks, query_scales, key_blocks, value_bloc...  13.9 us
    ppermute x3, starting transfers between devices, collect(): upper.append(lax.ppermute(upper[-1] if upper else value, axis, back))  12.9 us
    unnamed x20, local copies, waits for them, and re-layouts  9.93 us
    all_to_all x3, local copies, waits for them, and re-layouts, local(): lax.all_to_all(merged, 'ulysses', split_axis=0, concat_axis=1, tiled=True)  8.94 us
  transfers between devices with their start and end apart: 9, of which 3 were waited for; matrix products, arithmetic and copies ran while one was open for 15% of the time, Pallas kernels for 0%

profile of v1, /device:TPU:0, one launch (start us, length us, event | category | flops | bytes accessed | tf_op | source)
XLA Modules:
  0.0 219.7 jit_solution(13252557533301178345)
XLA Ops:
  6.5 1.3 copy.61
  7.8 3.9 %all_to_all.73 = bf16[128,2,512]{0,2,1:T(8,128)(2,1)S(1)} all-to-all(bf16[128,2,512]{0,2,1:T(8,128)(2,1)S(1)} %bitcast.177), channel_id=1, replica_groups=mesh['group'=2,'blk'=8,'ulysses'=2] {'ulysses'}, dimensions={1} | all-to-all | bytes 524288 | tf_op jit(solution)/shard_map/all_to_all | solution.py:97
  11.9 3.0 %collective-permute-start = (bf16[256,512]{1,0:T(8,128)(2,1)S(1)}, bf16[256,512]{1,0:T(8,128)(2,1)S(1)}, u32[]{:S(2)}, u32[]{:S(2)}) collective-permute-start(bf16[256,512]{1,0:T(8,128)(2,1)S(1)} %bitcast.172), channel_id=1, source_target_pairs={{0,2},{2,4},{4,6},{6,8},{8,10},{10,12},{12,14},{14,0},{1,3},{3,5},... | collective-permute-start | bytes 786440 | tf_op jit(solution)/shard_map/ppermute | solution.py:24
  15.0 3.1 %collective-permute-start.4 = (bf16[256,512]{1,0:T(8,128)(2,1)S(1)}, bf16[256,512]{1,0:T(8,128)(2,1)S(1)}, u32[]{:S(2)}, u32[]{:S(2)}) collective-permute-start(bf16[256,512]{1,0:T(8,128)(2,1)S(1)} %bitcast.173), channel_id=1, source_target_pairs={{2,0},{4,2},{6,4},{8,6},{10,8},{12,10},{14,12},{0,14},{3,1},{5,3},... | collective-permute-start | bytes 786440 | tf_op jit(solution)/shard_map/ppermute | solution.py:26
  18.1 1.1 copy.66
  19.2 3.9 %all_to_all.74 = bf16[128,2,512]{0,2,1:T(8,128)(2,1)S(1)} all-to-all(bf16[128,2,512]{0,2,1:T(8,128)(2,1)S(1)} %bitcast.178), channel_id=1, replica_groups=mesh['group'=2,'blk'=8,'ulysses'=2] {'ulysses'}, dimensions={1} | all-to-all | bytes 524288 | tf_op jit(solution)/shard_map/all_to_all | solution.py:98
  24.0 2.4 %copy.60 = bf16[128,8192]{0,1:T(8,128)(2,1)} copy(bf16[128,8192]{1,0:T(8,128)(2,1)S(1)} %copy-done.1) | data formatting | bytes 4194304 | tf_op args[0]
  26.5 5.0 %all-to-all-start = ((bf16[128,2,4096]{0,2,1:T(8,128)(2,1)}), bf16[128,2,4096]{0,2,1:T(8,128)(2,1)}, u32[]{:S(2)}, u32[]{:S(2)}) async-start(bf16[128,2,4096]{0,2,1:T(8,128)(2,1)} %bitcast.27), calls=%async_computation | async-start | bytes 4194304 | tf_op jit(solution)/shard_map/all_to_all | solution.py:96
  32.3 17.2 %collective-permute-done.1 = bf16[256,512]{1,0:T(8,128)(2,1)S(1)} collective-permute-done((bf16[256,512]{1,0:T(8,128)(2,1)S(1)}, bf16[256,512]{1,0:T(8,128)(2,1)S(1)}, u32[]{:S(2)}, u32[]{:S(2)}) %collective-permute-start.1) | collective-permute-done | bytes 262176 | tf_op jit(solution)/shard_map/ppermute | solution.py:24
  49.6 4.8 %collective-permute-start.5 = (bf16[256,512]{1,0:T(8,128)(2,1)S(1)}, bf16[256,512]{1,0:T(8,128)(2,1)S(1)}, u32[]{:S(2)}, u32[]{:S(2)}) collective-permute-start(bf16[256,512]{1,0:T(8,128)(2,1)S(1)} %collective-permute-done.4), channel_id=1, source_target_pairs={{2,0},{4,2},{6,4},{8,6},{10,8},{12,10},{14,12},{0,14},{3,1},{5,3},... | collective-permute-start | bytes 786440 | tf_op jit(solution)/shard_map/ppermute | solution.py:26
  54.4 11.8 %collective-permute-done.2 = bf16[256,512]{1,0:T(8,128)(2,1)S(1)} collective-permute-done((bf16[256,512]{1,0:T(8,128)(2,1)S(1)}, bf16[256,512]{1,0:T(8,128)(2,1)S(1)}, u32[]{:S(2)}, u32[]{:S(2)}) %collective-permute-start.2) | collective-permute-done | bytes 262176 | tf_op jit(solution)/shard_map/ppermute | solution.py:24
  66.1 2.5 %collective-permute-start.3 = (bf16[256,512]{1,0:T(8,128)(2,1)S(1)}, bf16[256,512]{1,0:T(8,128)(2,1)S(1)}, u32[]{:S(2)}, u32[]{:S(2)}) collective-permute-start(bf16[256,512]{1,0:T(8,128)(2,1)S(1)} %collective-permute-done.2), channel_id=1, source_target_pairs={{0,2},{2,4},{4,6},{6,8},{8,10},{10,12},{12,14},{14,0},{1,3},{3,5},... | collective-permute-start | bytes 786440 | tf_op jit(solution)/shard_map/ppermute | solution.py:24
  68.9 1.5 gather_fusion.3
  70.6 5.1 %collective-permute-start.6 = (bf16[256,512]{1,0:T(8,128)(2,1)S(1)}, bf16[256,512]{1,0:T(8,128)(2,1)S(1)}, u32[]{:S(2)}, u32[]{:S(2)}) collective-permute-start(bf16[256,512]{1,0:T(8,128)(2,1)S(1)} %collective-permute-done.5), channel_id=1, source_target_pairs={{2,0},{4,2},{6,4},{8,6},{10,8},{12,10},{14,12},{0,14},{3,1},{5,3},... | collective-permute-start | bytes 786440 | tf_op jit(solution)/shard_map/ppermute | solution.py:26
  75.7 7.3 %collective-permute-done.3 = bf16[256,512]{1,0:T(8,128)(2,1)S(1)} collective-permute-done((bf16[256,512]{1,0:T(8,128)(2,1)S(1)}, bf16[256,512]{1,0:T(8,128)(2,1)S(1)}, u32[]{:S(2)}, u32[]{:S(2)}) %collective-permute-start.3) | collective-permute-done | bytes 262176 | tf_op jit(solution)/shard_map/ppermute | solution.py:24
  88.8 2.3 %gather_fusion = bf16[8,256,512]{2,1,0:T(8,128)(2,1)S(1)} fusion(bf16[8,256,512]{2,1,0:T(8,128)(2,1)} %bitcast_dynamic-update-slice_fusion.1, s32[1024]{0:T(1024)S(1)} %pad_clamp_fusion), kind=kCustom, calls=%fused_computation | custom fusion | bytes 4194336 | tf_op jit(solution)/shard_map/gather | solution.py:29
  91.1 2.1 reshape.195
  93.2 2.1 copy.65
  95.4 3.1 %gather_fusion.1 = bf16[128,128,128]{2,1,0:T(8,128)(2,1)} fusion(bf16[16,128,4,128]{3,1,2,0:T(8,128)(2,1)S(1)} %copy.65, s32[128]{0:T(128)S(1)} %reshape.172), kind=kCustom, calls=%fused_computation.1 | custom fusion | bytes 8389632 | tf_op jit(solution)/shard_map/gather | solution.py:52
  98.5 4.0 %reshape.196 = bf16[16,128,4,128]{3,2,1,0:T(4,128)(2,1)} reshape(bf16[2048,512]{1,0:T(8,128)(2,1)} %all-gather.2.cloned.1.call-done) | data formatting | bytes 4194304 | tf_op jit(solution)/shard_map/reshape | solution.py:50
  102.5 2.1 copy.69
  104.7 3.1 %gather_fusion.2 = bf16[128,128,128]{2,1,0:T(8,128)(2,1)} fusion(bf16[16,128,4,128]{3,1,2,0:T(8,128)(2,1)S(1)} %copy.69, s32[128]{0:T(128)S(1)} %reshape.172), kind=kCustom, calls=%fused_computation.2 | custom fusion | bytes 8389632 | tf_op jit(solution)/shard_map/gather | solution.py:52
  107.8 89.8 %while.21 = (s32[]{:T(128)}, bf16[2,128,4,8,128]{1,4,3,2,0:T(8,128)(2,1)}, bf16[2,128,4,8,128]{1,4,3,2,0:T(8,128)(2,1)}, f32[2,4,8]{2,1,0:T(4,128)S(1)}, bf16[2,...) while((s32[]{:T(128)}, ...), condition=%wide.region_6.7_spmd, body=%wide.region_1.6_spmd.sunk | while | flops 1108097024 | bytes 46721236 | solution.py:125
  107.8 1.7 constant_dynamic-slice_fusion.13
  109.5 2.6 %copy.88 = bf16[1,4,16,128,128]{3,4,2,1,0:T(8,128)(2,1)} copy(bf16[1,4,16,128,128]{4,3,2,1,0:T(8,128)(2,1)S(1)} %constant_dynamic-slice_fusion.13) | data formatting | bytes 4194304 | tf_op jit(solution)/shard_map/while/body/jit(dynamic_index_in_dim)/dynamic_slice | solution.py:125
  112.1 1.3 constant_dynamic-slice_fusion.14
  113.4 1.3 copy.89
  114.8 1.7 dynamic-slice_bitcast_fusion.6
  116.5 35.1 %while.22 = (s32[]{:T(128)}, bf16[4,128,8,128]{1,3,2,0:T(8,128)(2,1)S(1)}, bf16[4,16,128,128]{2,3,1,0:T(8,128)(2,1)}, pred[4,16]{1,0:T(4,128)(4,1)S(1)}, pred[4,...) while((s32[]{:T(128)}, ...), condition=%wide.region_5.5_spmd, body=%wide.region_2.4_spmd.sunk | while | flops 1108097024 | bytes 27845104 | solution.py:79
  116.9 2.4 %fusion.60 = (f32[8,128]{1,0:T(8,128)S(1)}, f32[16,128,128,8]{2,1,3,0:T(8,128)S(1)}) fusion(f32[16]{0:T(128)S(1)} %fusion.57, f32[8]{0:T(128)S(1)} %fusion.58, pred[128,16,128]{0,2,1:T(8,128)(4,1)S(1)} %or_and_fusion.2, bf16[4,128,8,128]{3,1,2,0:T(8,128)(2,1)} %get-tuple-element.362, s32[]{:T(128)} %get-tuple-element.346, ...), kind=kOutput, calls=%fused_computation.8.clone.1 | convolution fusion | flops 545258496 | bytes 9443328 | tf_op jit(solution)/shard_map/while/body/eval_jaxpr/while/body/eval_jaxpr/tpd,nsd->ptns/dot_general | solution.py:57
  119.3 2.4 %fusion.61 = f32[8,128]{1,0:T(8,128)S(1)} fusion(f32[16,128,128,8]{2,1,3,0:T(8,128)S(1)} %get-tuple-element.334, f32[8,128]{1,0:T(8,128)S(1)} %get-tuple-element.335, f32[16]{0:T(128)S(1)} %fusion.57, f32[8]{0:T(128)S(1)} %fusion.58, pred[128,16,128]{0,2,1:T(8,128)(4,1)S(1)} %or_and_fusion.2), kind=kLoop, calls=%fused_computation.6.clone.1 | loop fusion | flops 12581888 | bytes 8659040 | tf_op jit(solution)/shard_map/while/body/eval_jaxpr/while/body/eval_jaxpr/reduce_sum | solution.py:67
  121.7 3.6 %fusion.62 = bf16[4,128,8,128]{1,3,2,0:T(8,128)(2,1)S(1)} fusion(bf16[4,128,8,128]{1,3,2,0:T(8,128)(2,1)S(1)} %get-tuple-element.347, s32[]{:T(128)} %get-tuple-element.346, f32[16,128,128,8]{2,1,3,0:T(8,128)S(1)} %get-tuple-element.334, f32[8,128]{1,0:T(8,128)S(1)} %get-tuple-element.335, f32[16]{0:T(128)S(1)} %fusion.57, f32[8]{0:T(128)S(1)} %fusion.58, ...), kind=kOutput, calls=%fused_computation.15.clone.1 | convolution fusion | flops 549715968 | bytes 9447424 | tf_op jit(solution)/shard_map/while/body/eval_jaxpr/while/body/eval_jaxpr/ptns,nsd->tpd/dot_general | solution.py:68
  125.6 2.4 %fusion.60 = (f32[8,128]{1,0:T(8,128)S(1)}, f32[16,128,128,8]{2,1,3,0:T(8,128)S(1)}) fusion(f32[16]{0:T(128)S(1)} %fusion.57, f32[8]{0:T(128)S(1)} %fusion.58, pred[128,16,128]{0,2,1:T(8,128)(4,1)S(1)} %or_and_fusion.2, bf16[4,128,8,128]{3,1,2,0:T(8,128)(2,1)} %get-tuple-element.362, s32[]{:T(128)} %get-tuple-element.346, ...), kind=kOutput, calls=%fused_computation.8.clone.1 | convolution fusion | flops 545258496 | bytes 9443328 | tf_op jit(solution)/shard_map/while/body/eval_jaxpr/while/body/eval_jaxpr/tpd,nsd->ptns/dot_general | solution.py:57
  128.0 2.4 %fusion.61 = f32[8,128]{1,0:T(8,128)S(1)} fusion(f32[16,128,128,8]{2,1,3,0:T(8,128)S(1)} %get-tuple-element.334, f32[8,128]{1,0:T(8,128)S(1)} %get-tuple-element.335, f32[16]{0:T(128)S(1)} %fusion.57, f32[8]{0:T(128)S(1)} %fusion.58, pred[128,16,128]{0,2,1:T(8,128)(4,1)S(1)} %or_and_fusion.2), kind=kLoop, calls=%fused_computation.6.clone.1 | loop fusion | flops 12581888 | bytes 8659040 | tf_op jit(solution)/shard_map/while/body/eval_jaxpr/while/body/eval_jaxpr/reduce_sum | solution.py:67
  130.5 3.6 %fusion.62 = bf16[4,128,8,128]{1,3,2,0:T(8,128)(2,1)S(1)} fusion(bf16[4,128,8,128]{1,3,2,0:T(8,128)(2,1)S(1)} %get-tuple-element.347, s32[]{:T(128)} %get-tuple-element.346, f32[16,128,128,8]{2,1,3,0:T(8,128)S(1)} %get-tuple-element.334, f32[8,128]{1,0:T(8,128)S(1)} %get-tuple-element.335, f32[16]{0:T(128)S(1)} %fusion.57, f32[8]{0:T(128)S(1)} %fusion.58, ...), kind=kOutput, calls=%fused_computation.15.clone.1 | convolution fusion | flops 549715968 | bytes 9447424 | tf_op jit(solution)/shard_map/while/body/eval_jaxpr/while/body/eval_jaxpr/ptns,nsd->tpd/dot_general | solution.py:68
  134.4 2.4 %fusion.60 = (f32[8,128]{1,0:T(8,128)S(1)}, f32[16,128,128,8]{2,1,3,0:T(8,128)S(1)}) fusion(f32[16]{0:T(128)S(1)} %fusion.57, f32[8]{0:T(128)S(1)} %fusion.58, pred[128,16,128]{0,2,1:T(8,128)(4,1)S(1)} %or_and_fusion.2, bf16[4,128,8,128]{3,1,2,0:T(8,128)(2,1)} %get-tuple-element.362, s32[]{:T(128)} %get-tuple-element.346, ...), kind=kOutput, calls=%fused_computation.8.clone.1 | convolution fusion | flops 545258496 | bytes 9443328 | tf_op jit(solution)/shard_map/while/body/eval_jaxpr/while/body/eval_jaxpr/tpd,nsd->ptns/dot_general | solution.py:57
  136.8 2.4 %fusion.61 = f32[8,128]{1,0:T(8,128)S(1)} fusion(f32[16,128,128,8]{2,1,3,0:T(8,128)S(1)} %get-tuple-element.334, f32[8,128]{1,0:T(8,128)S(1)} %get-tuple-element.335, f32[16]{0:T(128)S(1)} %fusion.57, f32[8]{0:T(128)S(1)} %fusion.58, pred[128,16,128]{0,2,1:T(8,128)(4,1)S(1)} %or_and_fusion.2), kind=kLoop, calls=%fused_computation.6.clone.1 | loop fusion | flops 12581888 | bytes 8659040 | tf_op jit(solution)/shard_map/while/body/eval_jaxpr/while/body/eval_jaxpr/reduce_sum | solution.py:67
  139.2 3.6 %fusion.62 = bf16[4,128,8,128]{1,3,2,0:T(8,128)(2,1)S(1)} fusion(bf16[4,128,8,128]{1,3,2,0:T(8,128)(2,1)S(1)} %get-tuple-element.347, s32[]{:T(128)} %get-tuple-element.346, f32[16,128,128,8]{2,1,3,0:T(8,128)S(1)} %get-tuple-element.334, f32[8,128]{1,0:T(8,128)S(1)} %get-tuple-element.335, f32[16]{0:T(128)S(1)} %fusion.57, f32[8]{0:T(128)S(1)} %fusion.58, ...), kind=kOutput, calls=%fused_computation.15.clone.1 | convolution fusion | flops 549715968 | bytes 9447424 | tf_op jit(solution)/shard_map/while/body/eval_jaxpr/while/body/eval_jaxpr/ptns,nsd->tpd/dot_general | solution.py:68
  143.2 2.4 %fusion.60 = (f32[8,128]{1,0:T(8,128)S(1)}, f32[16,128,128,8]{2,1,3,0:T(8,128)S(1)}) fusion(f32[16]{0:T(128)S(1)} %fusion.57, f32[8]{0:T(128)S(1)} %fusion.58, pred[128,16,128]{0,2,1:T(8,128)(4,1)S(1)} %or_and_fusion.2, bf16[4,128,8,128]{3,1,2,0:T(8,128)(2,1)} %get-tuple-element.362, s32[]{:T(128)} %get-tuple-element.346, ...), kind=kOutput, calls=%fused_computation.8.clone.1 | convolution fusion | flops 545258496 | bytes 9443328 | tf_op jit(solution)/shard_map/while/body/eval_jaxpr/while/body/eval_jaxpr/tpd,nsd->ptns/dot_general | solution.py:57
  145.6 2.4 %fusion.61 = f32[8,128]{1,0:T(8,128)S(1)} fusion(f32[16,128,128,8]{2,1,3,0:T(8,128)S(1)} %get-tuple-element.334, f32[8,128]{1,0:T(8,128)S(1)} %get-tuple-element.335, f32[16]{0:T(128)S(1)} %fusion.57, f32[8]{0:T(128)S(1)} %fusion.58, pred[128,16,128]{0,2,1:T(8,128)(4,1)S(1)} %or_and_fusion.2), kind=kLoop, calls=%fused_computation.6.clone.1 | loop fusion | flops 12581888 | bytes 8659040 | tf_op jit(solution)/shard_map/while/body/eval_jaxpr/while/body/eval_jaxpr/reduce_sum | solution.py:67
  148.0 3.6 %fusion.62 = bf16[4,128,8,128]{1,3,2,0:T(8,128)(2,1)S(1)} fusion(bf16[4,128,8,128]{1,3,2,0:T(8,128)(2,1)S(1)} %get-tuple-element.347, s32[]{:T(128)} %get-tuple-element.346, f32[16,128,128,8]{2,1,3,0:T(8,128)S(1)} %get-tuple-element.334, f32[8,128]{1,0:T(8,128)S(1)} %get-tuple-element.335, f32[16]{0:T(128)S(1)} %fusion.57, f32[8]{0:T(128)S(1)} %fusion.58, ...), kind=kOutput, calls=%fused_computation.15.clone.1 | convolution fusion | flops 549715968 | bytes 9447424 | tf_op jit(solution)/shard_map/while/body/eval_jaxpr/while/body/eval_jaxpr/ptns,nsd->tpd/dot_general | solution.py:68
  151.6 1.0 bitcast_dynamic-update-slice_fusion.10
  152.7 1.7 constant_dynamic-slice_fusion.13
  154.4 2.6 %copy.88 = bf16[1,4,16,128,128]{3,4,2,1,0:T(8,128)(2,1)} copy(bf16[1,4,16,128,128]{4,3,2,1,0:T(8,128)(2,1)S(1)} %constant_dynamic-slice_fusion.13) | data formatting | bytes 4194304 | tf_op jit(solution)/shard_map/while/body/jit(dynamic_index_in_dim)/dynamic_slice | solution.py:125
  157.0 1.3 constant_dynamic-slice_fusion.14
  158.3 1.3 copy.89
  159.7 1.7 dynamic-slice_bitcast_fusion.6
  161.4 35.1 %while.22 = (s32[]{:T(128)}, bf16[4,128,8,128]{1,3,2,0:T(8,128)(2,1)S(1)}, bf16[4,16,128,128]{2,3,1,0:T(8,128)(2,1)}, pred[4,16]{1,0:T(4,128)(4,1)S(1)}, pred[4,...) while((s32[]{:T(128)}, ...), condition=%wide.region_5.5_spmd, body=%wide.region_2.4_spmd.sunk | while | flops 1108097024 | bytes 27845104 | solution.py:79
  161.8 2.4 %fusion.60 = (f32[8,128]{1,0:T(8,128)S(1)}, f32[16,128,128,8]{2,1,3,0:T(8,128)S(1)}) fusion(f32[16]{0:T(128)S(1)} %fusion.57, f32[8]{0:T(128)S(1)} %fusion.58, pred[128,16,128]{0,2,1:T(8,128)(4,1)S(1)} %or_and_fusion.2, bf16[4,128,8,128]{3,1,2,0:T(8,128)(2,1)} %get-tuple-element.362, s32[]{:T(128)} %get-tuple-element.346, ...), kind=kOutput, calls=%fused_computation.8.clone.1 | convolution fusion | flops 545258496 | bytes 9443328 | tf_op jit(solution)/shard_map/while/body/eval_jaxpr/while/body/eval_jaxpr/tpd,nsd->ptns/dot_general | solution.py:57
  164.2 2.4 %fusion.61 = f32[8,128]{1,0:T(8,128)S(1)} fusion(f32[16,128,128,8]{2,1,3,0:T(8,128)S(1)} %get-tuple-element.334, f32[8,128]{1,0:T(8,128)S(1)} %get-tuple-element.335, f32[16]{0:T(128)S(1)} %fusion.57, f32[8]{0:T(128)S(1)} %fusion.58, pred[128,16,128]{0,2,1:T(8,128)(4,1)S(1)} %or_and_fusion.2), kind=kLoop, calls=%fused_computation.6.clone.1 | loop fusion | flops 12581888 | bytes 8659040 | tf_op jit(solution)/shard_map/while/body/eval_jaxpr/while/body/eval_jaxpr/reduce_sum | solution.py:67
  166.6 3.6 %fusion.62 = bf16[4,128,8,128]{1,3,2,0:T(8,128)(2,1)S(1)} fusion(bf16[4,128,8,128]{1,3,2,0:T(8,128)(2,1)S(1)} %get-tuple-element.347, s32[]{:T(128)} %get-tuple-element.346, f32[16,128,128,8]{2,1,3,0:T(8,128)S(1)} %get-tuple-element.334, f32[8,128]{1,0:T(8,128)S(1)} %get-tuple-element.335, f32[16]{0:T(128)S(1)} %fusion.57, f32[8]{0:T(128)S(1)} %fusion.58, ...), kind=kOutput, calls=%fused_computation.15.clone.1 | convolution fusion | flops 549715968 | bytes 9447424 | tf_op jit(solution)/shard_map/while/body/eval_jaxpr/while/body/eval_jaxpr/ptns,nsd->tpd/dot_general | solution.py:68
  170.5 2.4 %fusion.60 = (f32[8,128]{1,0:T(8,128)S(1)}, f32[16,128,128,8]{2,1,3,0:T(8,128)S(1)}) fusion(f32[16]{0:T(128)S(1)} %fusion.57, f32[8]{0:T(128)S(1)} %fusion.58, pred[128,16,128]{0,2,1:T(8,128)(4,1)S(1)} %or_and_fusion.2, bf16[4,128,8,128]{3,1,2,0:T(8,128)(2,1)} %get-tuple-element.362, s32[]{:T(128)} %get-tuple-element.346, ...), kind=kOutput, calls=%fused_computation.8.clone.1 | convolution fusion | flops 545258496 | bytes 9443328 | tf_op jit(solution)/shard_map/while/body/eval_jaxpr/while/body/eval_jaxpr/tpd,nsd->ptns/dot_general | solution.py:57
  173.0 2.4 %fusion.61 = f32[8,128]{1,0:T(8,128)S(1)} fusion(f32[16,128,128,8]{2,1,3,0:T(8,128)S(1)} %get-tuple-element.334, f32[8,128]{1,0:T(8,128)S(1)} %get-tuple-element.335, f32[16]{0:T(128)S(1)} %fusion.57, f32[8]{0:T(128)S(1)} %fusion.58, pred[128,16,128]{0,2,1:T(8,128)(4,1)S(1)} %or_and_fusion.2), kind=kLoop, calls=%fused_computation.6.clone.1 | loop fusion | flops 12581888 | bytes 8659040 | tf_op jit(solution)/shard_map/while/body/eval_jaxpr/while/body/eval_jaxpr/reduce_sum | solution.py:67
  175.4 3.6 %fusion.62 = bf16[4,128,8,128]{1,3,2,0:T(8,128)(2,1)S(1)} fusion(bf16[4,128,8,128]{1,3,2,0:T(8,128)(2,1)S(1)} %get-tuple-element.347, s32[]{:T(128)} %get-tuple-element.346, f32[16,128,128,8]{2,1,3,0:T(8,128)S(1)} %get-tuple-element.334, f32[8,128]{1,0:T(8,128)S(1)} %get-tuple-element.335, f32[16]{0:T(128)S(1)} %fusion.57, f32[8]{0:T(128)S(1)} %fusion.58, ...), kind=kOutput, calls=%fused_computation.15.clone.1 | convolution fusion | flops 549715968 | bytes 9447424 | tf_op jit(solution)/shard_map/while/body/eval_jaxpr/while/body/eval_jaxpr/ptns,nsd->tpd/dot_general | solution.py:68
  179.3 2.4 %fusion.60 = (f32[8,128]{1,0:T(8,128)S(1)}, f32[16,128,128,8]{2,1,3,0:T(8,128)S(1)}) fusion(f32[16]{0:T(128)S(1)} %fusion.57, f32[8]{0:T(128)S(1)} %fusion.58, pred[128,16,128]{0,2,1:T(8,128)(4,1)S(1)} %or_and_fusion.2, bf16[4,128,8,128]{3,1,2,0:T(8,128)(2,1)} %get-tuple-element.362, s32[]{:T(128)} %get-tuple-element.346, ...), kind=kOutput, calls=%fused_computation.8.clone.1 | convolution fusion | flops 545258496 | bytes 9443328 | tf_op jit(solution)/shard_map/while/body/eval_jaxpr/while/body/eval_jaxpr/tpd,nsd->ptns/dot_general | solution.py:57
  181.7 2.4 %fusion.61 = f32[8,128]{1,0:T(8,128)S(1)} fusion(f32[16,128,128,8]{2,1,3,0:T(8,128)S(1)} %get-tuple-element.334, f32[8,128]{1,0:T(8,128)S(1)} %get-tuple-element.335, f32[16]{0:T(128)S(1)} %fusion.57, f32[8]{0:T(128)S(1)} %fusion.58, pred[128,16,128]{0,2,1:T(8,128)(4,1)S(1)} %or_and_fusion.2), kind=kLoop, calls=%fused_computation.6.clone.1 | loop fusion | flops 12581888 | bytes 8659040 | tf_op jit(solution)/shard_map/while/body/eval_jaxpr/while/body/eval_jaxpr/reduce_sum | solution.py:67
  184.2 3.6 %fusion.62 = bf16[4,128,8,128]{1,3,2,0:T(8,128)(2,1)S(1)} fusion(bf16[4,128,8,128]{1,3,2,0:T(8,128)(2,1)S(1)} %get-tuple-element.347, s32[]{:T(128)} %get-tuple-element.346, f32[16,128,128,8]{2,1,3,0:T(8,128)S(1)} %get-tuple-element.334, f32[8,128]{1,0:T(8,128)S(1)} %get-tuple-element.335, f32[16]{0:T(128)S(1)} %fusion.57, f32[8]{0:T(128)S(1)} %fusion.58, ...), kind=kOutput, calls=%fused_computation.15.clone.1 | convolution fusion | flops 549715968 | bytes 9447424 | tf_op jit(solution)/shard_map/while/body/eval_jaxpr/while/body/eval_jaxpr/ptns,nsd->tpd/dot_general | solution.py:68
  188.1 2.4 %fusion.60 = (f32[8,128]{1,0:T(8,128)S(1)}, f32[16,128,128,8]{2,1,3,0:T(8,128)S(1)}) fusion(f32[16]{0:T(128)S(1)} %fusion.57, f32[8]{0:T(128)S(1)} %fusion.58, pred[128,16,128]{0,2,1:T(8,128)(4,1)S(1)} %or_and_fusion.2, bf16[4,128,8,128]{3,1,2,0:T(8,128)(2,1)} %get-tuple-element.362, s32[]{:T(128)} %get-tuple-element.346, ...), kind=kOutput, calls=%fused_computation.8.clone.1 | convolution fusion | flops 545258496 | bytes 9443328 | tf_op jit(solution)/shard_map/while/body/eval_jaxpr/while/body/eval_jaxpr/tpd,nsd->ptns/dot_general | solution.py:57
  190.5 2.4 %fusion.61 = f32[8,128]{1,0:T(8,128)S(1)} fusion(f32[16,128,128,8]{2,1,3,0:T(8,128)S(1)} %get-tuple-element.334, f32[8,128]{1,0:T(8,128)S(1)} %get-tuple-element.335, f32[16]{0:T(128)S(1)} %fusion.57, f32[8]{0:T(128)S(1)} %fusion.58, pred[128,16,128]{0,2,1:T(8,128)(4,1)S(1)} %or_and_fusion.2), kind=kLoop, calls=%fused_computation.6.clone.1 | loop fusion | flops 12581888 | bytes 8659040 | tf_op jit(solution)/shard_map/while/body/eval_jaxpr/while/body/eval_jaxpr/reduce_sum | solution.py:67
  192.9 3.6 %fusion.62 = bf16[4,128,8,128]{1,3,2,0:T(8,128)(2,1)S(1)} fusion(bf16[4,128,8,128]{1,3,2,0:T(8,128)(2,1)S(1)} %get-tuple-element.347, s32[]{:T(128)} %get-tuple-element.346, f32[16,128,128,8]{2,1,3,0:T(8,128)S(1)} %get-tuple-element.334, f32[8,128]{1,0:T(8,128)S(1)} %get-tuple-element.335, f32[16]{0:T(128)S(1)} %fusion.57, f32[8]{0:T(128)S(1)} %fusion.58, ...), kind=kOutput, calls=%fused_computation.15.clone.1 | convolution fusion | flops 549715968 | bytes 9447424 | tf_op jit(solution)/shard_map/while/body/eval_jaxpr/while/body/eval_jaxpr/ptns,nsd->tpd/dot_general | solution.py:68
  197.6 2.9 %copy.83 = bf16[2,128,4096]{2,1,0:T(8,128)(2,1)S(1)} copy(bf16[2,128,4096]{1,2,0:T(8,128)(2,1)} %bitcast.170) | data formatting | bytes 4194304 | tf_op jit(solution)/shard_map/all_to_all | solution.py:130
  200.5 6.3 %all_to_all.75 = bf16[2,128,4096]{2,1,0:T(8,128)(2,1)} all-to-all(bf16[2,128,4096]{2,1,0:T(8,128)(2,1)S(1)} %copy.83), channel_id=1, replica_groups=mesh['group'=2,'blk'=8,'ulysses'=2] {'ulysses'}, dimensions={0} | all-to-all | bytes 4194304 | tf_op jit(solution)/shard_map/all_to_all | solution.py:130
  206.8 3.1 %copy.73 = bf16[2,128,4096]{1,2,0:T(8,128)(2,1)S(1)} copy(bf16[2,128,4096]{2,1,0:T(8,128)(2,1)} %all_to_all.75) | data formatting | bytes 4194304 | tf_op jit(solution)/shard_map/all_to_all | solution.py:130
  210.0 2.9 %copy.74 = bf16[128,8192]{1,0:T(8,128)(2,1)} copy(bf16[128,8192]{0,1:T(8,128)(2,1)S(1)} %bitcast.168) | data formatting | bytes 4194304 | tf_op jit(solution)/shard_map/all_to_all | solution.py:130
  (99 shorter events, 11.5 us)
Async XLA Ops:
  6.5 62.3 %copy-start = (bf16[16,8]{0,1:T(8,128)(2,1)S(1)}, bf16[16,8]{0,1:T(8,128)(2,1)}, u32[]{:S(2)}) copy-start(bf16[16,8]{0,1:T(8,128)(2,1)} %param.15) | copy-start | bytes 772
  6.5 17.5 %copy-start.1 = (bf16[128,8192]{1,0:T(8,128)(2,1)S(1)}, bf16[128,8192]{1,0:T(8,128)(2,1)}, u32[]{:S(2)}) copy-start(bf16[128,8192]{1,0:T(8,128)(2,1)} %param.11) | copy-start | bytes 6291460
  6.5 91.9 %all-gather.2.cloned.1.call-start = ((), (), s32[]{:S(2)}) async-start(), calls=%async_computation.4 | async-start | bytes 2359296 | tf_op jit(solution)/shard_map/all_gather | solution.py:119
  11.9 20.2 %collective-permute-start = (bf16[256,512]{1,0:T(8,128)(2,1)S(1)}, bf16[256,512]{1,0:T(8,128)(2,1)S(1)}, u32[]{:S(2)}, u32[]{:S(2)}) collective-permute-start(bf16[256,512]{1,0:T(8,128)(2,1)S(1)} %bitcast.172), channel_id=1, source_target_pairs={{0,2},{2,4},{4,6},{6,8},{8,10},{10,12},{12,14},{14,0},{1,3},{3,5},... | collective-permute-start | bytes 786440 | tf_op jit(solution)/shard_map/ppermute | solution.py:24
  15.0 34.6 %collective-permute-start.4 = (bf16[256,512]{1,0:T(8,128)(2,1)S(1)}, bf16[256,512]{1,0:T(8,128)(2,1)S(1)}, u32[]{:S(2)}, u32[]{:S(2)}) collective-permute-start(bf16[256,512]{1,0:T(8,128)(2,1)S(1)} %bitcast.173), channel_id=1, source_target_pairs={{2,0},{4,2},{6,4},{8,6},{10,8},{12,10},{14,12},{0,14},{3,1},{5,3},... | collective-permute-start | bytes 786440 | tf_op jit(solution)/shard_map/ppermute | solution.py:26
  26.5 5.1 %copy-start.2 = (s32[8,8]{1,0:T(8,128)S(1)}, s32[8,8]{1,0:T(8,128)}, u32[]{:S(2)}) copy-start(s32[8,8]{1,0:T(8,128)} %param.17) | copy-start | bytes 772
  26.5 5.1 %copy-start.3 = (s32[8,8]{1,0:T(8,128)S(1)}, s32[8,8]{1,0:T(8,128)}, u32[]{:S(2)}) copy-start(s32[8,8]{1,0:T(8,128)} %param.16) | copy-start | bytes 772
  26.5 42.1 %copy-start.4 = (bf16[2,64]{1,0:T(2,128)(2,1)S(1)}, bf16[2,64]{1,0:T(2,128)(2,1)}, u32[]{:S(2)}) copy-start(bf16[2,64]{1,0:T(2,128)(2,1)} %param.14) | copy-start | bytes 772
  26.5 81.3 %all-to-all-start = ((bf16[128,2,4096]{0,2,1:T(8,128)(2,1)}), bf16[128,2,4096]{0,2,1:T(8,128)(2,1)}, u32[]{:S(2)}, u32[]{:S(2)}) async-start(bf16[128,2,4096]{0,2,1:T(8,128)(2,1)} %bitcast.27), calls=%async_computation | async-start | bytes 4194304 | tf_op jit(solution)/shard_map/all_to_all | solution.py:96
  32.1 17.4 %collective-permute-start.1 = (bf16[256,512]{1,0:T(8,128)(2,1)S(1)}, bf16[256,512]{1,0:T(8,128)(2,1)S(1)}, u32[]{:S(2)}, u32[]{:S(2)}) collective-permute-start(bf16[256,512]{1,0:T(8,128)(2,1)S(1)} %collective-permute-done), channel_id=1, source_target_pairs={{0,2},{2,4},{4,6},{6,8},{8,10},{10,12},{12,14},{14,0},{1,3},{3,5},... | collective-permute-start | bytes 786440 | tf_op jit(solution)/shard_map/ppermute | solution.py:24
  49.5 16.7 %collective-permute-start.2 = (bf16[256,512]{1,0:T(8,128)(2,1)S(1)}, bf16[256,512]{1,0:T(8,128)(2,1)S(1)}, u32[]{:S(2)}, u32[]{:S(2)}) collective-permute-start(bf16[256,512]{1,0:T(8,128)(2,1)S(1)} %collective-permute-done.1), channel_id=1, source_target_pairs={{0,2},{2,4},{4,6},{6,8},{8,10},{10,12},{12,14},{14,0},{1,3},{3,5},... | collective-permute-start | bytes 786440 | tf_op jit(solution)/shard_map/ppermute | solution.py:24
  49.6 21.0 %collective-permute-start.5 = (bf16[256,512]{1,0:T(8,128)(2,1)S(1)}, bf16[256,512]{1,0:T(8,128)(2,1)S(1)}, u32[]{:S(2)}, u32[]{:S(2)}) collective-permute-start(bf16[256,512]{1,0:T(8,128)(2,1)S(1)} %collective-permute-done.4), channel_id=1, source_target_pairs={{2,0},{4,2},{6,4},{8,6},{10,8},{12,10},{14,12},{0,14},{3,1},{5,3},... | collective-permute-start | bytes 786440 | tf_op jit(solution)/shard_map/ppermute | solution.py:26
  66.1 16.9 %collective-permute-start.3 = (bf16[256,512]{1,0:T(8,128)(2,1)S(1)}, bf16[256,512]{1,0:T(8,128)(2,1)S(1)}, u32[]{:S(2)}, u32[]{:S(2)}) collective-permute-start(bf16[256,512]{1,0:T(8,128)(2,1)S(1)} %collective-permute-done.2), channel_id=1, source_target_pairs={{0,2},{2,4},{4,6},{6,8},{8,10},{10,12},{12,14},{14,0},{1,3},{3,5},... | collective-permute-start | bytes 786440 | tf_op jit(solution)/shard_map/ppermute | solution.py:24
  70.6 17.5 %collective-permute-start.6 = (bf16[256,512]{1,0:T(8,128)(2,1)S(1)}, bf16[256,512]{1,0:T(8,128)(2,1)S(1)}, u32[]{:S(2)}, u32[]{:S(2)}) collective-permute-start(bf16[256,512]{1,0:T(8,128)(2,1)S(1)} %collective-permute-done.5), channel_id=1, source_target_pairs={{2,0},{4,2},{6,4},{8,6},{10,8},{12,10},{14,12},{0,14},{3,1},{5,3},... | collective-permute-start | bytes 786440 | tf_op jit(solution)/shard_map/ppermute | solution.py:26
Sparse Core Ops, SparseCore 0:
  24.2 66.1 all-gather.1
